TPU v7x, 32 devices: a whole 2x2x4 slice. The times are simulated.
32 devices in a mesh: parts: 2 (over y), brick: 4 (over z), tile: 2 (over x), depth: 2 (over core).
Axes of the slice: x: 2, y: 2, z: 4, core: 2. Of those that a mesh axis runs over, the one named last changes fastest.
Arguments:
- soot_extinction: bfloat16 [64, 64, 512], P(('brick', 'depth'), 'parts', 'tile'), parts along dimension 1, may hold values from 0.0099487305 to 1
- scaled_warmth: bfloat16 [64, 64, 512], P(('brick', 'depth'), 'parts', 'tile'), parts along dimension 1, may hold values from 0.5 to 2
- layer_nearness_position: int32 [16], P('parts'), parts along dimension 0, may hold values from 0 to 7, each once
Outputs:
- colour: float32 [3, 64, 512], P(None, ('parts', 'brick', 'tile', 'depth')), parts along dimension 1
- opacity: float32 [64, 512], P(('parts', 'brick', 'tile', 'depth')), parts along dimension 0
There are 2 independent parts, one for each index of `parts`. A program takes and returns all parts, laid end to end along the dimension named above; each array names one. Nothing has to cross between parts.
Inputs may be any that keep to these rules, and one draw needn't show every extreme that they name: layer_nearness_position holds each of 0 to 7 once.
All inputs are finite; a program needn't handle non-finite values.
Results may differ from a plain program's by a relative error of at most 0.0003.
Values sent between devices are 32-bit elements; how exact they have to be, the bound alone decides.
No kernel may reach another device: no remote copies, remote signals or barrier semaphores. Data moves between devices by JAX's collectives and lax.ppermute only.
A program may use at most 64 MiB of HBM per device.

v0:
```python
import functools

import jax
import jax.numpy as jnp
from jax import lax
from jax.experimental import pallas as pl
from jax.experimental.pallas import tpu as pltpu
from jax.sharding import PartitionSpec as P

GROUP = ("brick", "tile", "depth")
STEP_ROWS = 16


def march(step_rows, row_count, voxel_width, soot_ref, warmth_ref, out_ref):
    layers, rows, width = soot_ref.shape

    def strip(index, carry):
        top = pl.multiple_of(index * step_rows, step_rows)
        optical = jnp.zeros((step_rows, width), jnp.float32)
        transmit = jnp.ones((step_rows, width), jnp.float32)
        radiance = [jnp.zeros((step_rows, width), jnp.float32) for _ in range(3)]
        for k in range(layers):
            absorb = soot_ref[k, pl.ds(top, step_rows), :].astype(jnp.float32)
            glow = warmth_ref[k, pl.ds(top, step_rows), :].astype(jnp.float32)
            optical = optical + voxel_width * absorb
            passed = jnp.exp(-optical)
            root = jnp.exp(-0.5 / glow)
            square = root * root
            lost = square * (transmit - passed)
            transmit = passed
            radiance[0] = radiance[0] + lost
            radiance[1] = radiance[1] + lost * root
            radiance[2] = radiance[2] + lost * square
        fields = [2.0 * radiance[0], 2.0 * radiance[1], 2.0 * radiance[2], transmit]
        owners = step_rows // row_count
        for owner in range(owners):
            for c in range(4):
                out_ref[index * owners + owner, c * row_count : (c + 1) * row_count, :] = fields[c][
                    owner * row_count : (owner + 1) * row_count, :
                ]
        return carry

    steps = rows // step_rows
    lax.fori_loop(0, steps, strip, 0, unroll=steps <= 4)


def composite(bricks, tiles, cores, position_ref, pieces_ref, colour_ref, opacity_ref, slab_at):
    slabs = bricks * cores
    row_count, width = pieces_ref.shape[1] // 4, pieces_ref.shape[2]

    def place(s, carry):
        slab_at[position_ref[s]] = s
        return carry

    lax.fori_loop(0, slabs, place, 0, unroll=slabs <= 8)
    for tile in range(tiles):

        def add(p, state):
            colour, through = state
            slab = slab_at[p]
            piece = pieces_ref[((slab // cores) * tiles + tile) * cores + slab % cores]
            colour = [
                colour[c] + piece[c * row_count : (c + 1) * row_count] * through for c in range(3)
            ]
            return colour, through * piece[3 * row_count :]

        start = (
            [jnp.zeros((row_count, width), jnp.float32) for _ in range(3)],
            jnp.ones((row_count, width), jnp.float32),
        )
        colour, through = lax.fori_loop(0, slabs, add, start, unroll=slabs <= 8)
        columns = slice(tile * width, (tile + 1) * width)
        for c in range(3):
            colour_ref[c, :, columns] = colour[c]
        opacity_ref[:, columns] = 1.0 - through


def body(soot_extinction, scaled_warmth, layer_nearness_position):
    bricks, tiles, cores = (lax.axis_size(name) for name in GROUP)
    layers, rows, width = soot_extinction.shape
    slabs, owners = bricks * cores, bricks * tiles * cores
    row_count = rows // owners
    voxel_width = 12.0 / (layers * slabs)
    vmem = pl.BlockSpec(memory_space=pltpu.VMEM)
    pieces = pl.pallas_call(
        functools.partial(march, min(STEP_ROWS, rows), row_count, voxel_width),
        out_shape=jax.ShapeDtypeStruct((owners, 4 * row_count, width), jnp.float32),
        in_specs=[vmem, vmem],
        out_specs=vmem,
        name="march",
    )(soot_extinction, scaled_warmth)
    pieces = lax.all_to_all(pieces, GROUP, split_axis=0, concat_axis=0, tiled=True)
    return pl.pallas_call(
        functools.partial(composite, bricks, tiles, cores),
        out_shape=(
            jax.ShapeDtypeStruct((3, row_count, tiles * width), jnp.float32),
            jax.ShapeDtypeStruct((row_count, tiles * width), jnp.float32),
        ),
        in_specs=[pl.BlockSpec(memory_space=pltpu.SMEM), vmem],
        scratch_shapes=[pltpu.SMEM((slabs,), jnp.int32)],
        name="composite",
    )(layer_nearness_position, pieces)


def solution(mesh):
    placed = (
        P(("brick", "depth"), "parts", "tile"),
        P(("brick", "depth"), "parts", "tile"),
        P("parts"),
    )
    return jax.shard_map(
        body,
        mesh=mesh,
        in_specs=placed,
        out_specs=(
            P(None, ("parts",) + GROUP, None),
            P(("parts",) + GROUP, None),
        ),
        check_vma=False,
    )
```

profile of v0, /device:TPU:0, one launch (start us, length us, event | category | flops | bytes accessed | tf_op | source)
XLA Modules:
  0.0 19.4 jit_solution(17739154430177153589)
XLA Ops:
  0.6 1.8 %march.1 = f32[16,8,256]{2,1,0:T(8,128)} custom-call(bf16[8,32,256]{2,1,0:T(8,128)(2,1)} %soot_ref.1, bf16[8,32,256]{2,1,0:T(8,128)(2,1)} %warmth_ref.1), custom_call_target="tpu_custom_call" | custom-call | tf_op jit(solution)/shard_map/march/pallas_call | solution.py:85
  2.4 15.4 %all_to_all.5.pieces_ref = f32[16,8,256]{2,1,0:T(8,128)} all-to-all(f32[16,8,256]{2,1,0:T(8,128)} %march.1), channel_id=1, replica_groups=mesh['parts'=2,'brick'=4,'tile'=2,'depth'=2] {'brick','tile','depth'}, dimensions={0} | all-to-all | bytes 262144 | tf_op jit(solution)/shard_map/all_to_all | solution.py:92
  17.8 1.6 %composite.1 = (f32[3,2,512]{2,1,0:T(2,128)}, f32[2,512]{1,0:T(2,128)}) custom-call(s32[8]{0:T(128)} %position_ref.1, f32[16,8,256]{2,1,0:T(8,128)} %all_to_all.5.pieces_ref), custom_call_target="tpu_custom_call" | custom-call | tf_op jit(solution)/shard_map/composite/pallas_call | solution.py:93
where the time goes:
time: 19.6 us; the launch traced here: 19.4 us
  blocking collectives  15.4 us (79%)
  Pallas kernels  3.38 us (17%)
  between operations  0.63 us (3%)
    all_to_all x1, blocking collectives, body(): lax.all_to_all(pieces, GROUP, split_axis=0, concat_axis=0, tiled=True)  15.4 us
    pallas_call x1, Pallas kernels, body(): pl.pallas_call(functools.partial(march, min(STEP_ROWS, rows), row_count,...  1.78 us
    pallas_call x1, Pallas kernels, body(): pl.pallas_call(functools.partial(composite, bricks, tiles, cores), out_sh...  1.59 us

commit v1 on v0

--- a/solution.py
+++ b/solution.py
@@ -9,12 +9,30 @@
 
 GROUP = ("brick", "tile", "depth")
 STEP_ROWS = 16
+VMEM_BYTES = 24 << 20
 
 
-def march(step_rows, row_count, voxel_width, soot_ref, warmth_ref, out_ref):
+def march(step_rows, row_count, voxel_width, soot_hbm, warmth_hbm, out_ref, soot_ref, warmth_ref, arrived):
     layers, rows, width = soot_ref.shape
+    steps = rows // step_rows
+
+    def loads(index):
+        window = (slice(None), pl.ds(pl.multiple_of(index * step_rows, step_rows), step_rows))
+        return [
+            pltpu.make_async_copy(source.at[window], held.at[window], arrived.at[index, which])
+            for which, (source, held) in enumerate(
+                [(soot_hbm, soot_ref), (warmth_hbm, warmth_ref)]
+            )
+        ]
+
+    def fetch(index, carry):
+        for copy in loads(index):
+            copy.start()
+        return carry
 
     def strip(index, carry):
+        for copy in loads(index):
+            copy.wait()
         top = pl.multiple_of(index * step_rows, step_rows)
         optical = jnp.zeros((step_rows, width), jnp.float32)
         transmit = jnp.ones((step_rows, width), jnp.float32)
@@ -40,7 +58,7 @@
                 ]
         return carry
 
-    steps = rows // step_rows
+    lax.fori_loop(0, steps, fetch, 0, unroll=steps <= 4)
     lax.fori_loop(0, steps, strip, 0, unroll=steps <= 4)
 
 
@@ -81,14 +99,25 @@
     slabs, owners = bricks * cores, bricks * tiles * cores
     row_count = rows // owners
     voxel_width = 12.0 / (layers * slabs)
+    hbm = pl.BlockSpec(memory_space=pltpu.HBM)
     vmem = pl.BlockSpec(memory_space=pltpu.VMEM)
+    step_rows = min(STEP_ROWS, rows)
     pieces = pl.pallas_call(
-        functools.partial(march, min(STEP_ROWS, rows), row_count, voxel_width),
+        functools.partial(march, step_rows, row_count, voxel_width),
         out_shape=jax.ShapeDtypeStruct((owners, 4 * row_count, width), jnp.float32),
-        in_specs=[vmem, vmem],
+        in_specs=[hbm, hbm],
         out_specs=vmem,
+        scratch_shapes=[
+            pltpu.VMEM(soot_extinction.shape, soot_extinction.dtype),
+            pltpu.VMEM(scaled_warmth.shape, scaled_warmth.dtype),
+            pltpu.SemaphoreType.DMA((rows // step_rows, 2)),
+        ],
+        compiler_params=pltpu.CompilerParams(vmem_limit_bytes=VMEM_BYTES),
         name="march",
-    )(soot_extinction, scaled_warmth)
+    )(
+        pltpu.with_memory_space_constraint(soot_extinction, pltpu.HBM),
+        pltpu.with_memory_space_constraint(scaled_warmth, pltpu.HBM),
+    )
     pieces = lax.all_to_all(pieces, GROUP, split_axis=0, concat_axis=0, tiled=True)
     return pl.pallas_call(
         functools.partial(composite, bricks, tiles, cores),
@@ -98,6 +127,7 @@
         ),
         in_specs=[pl.BlockSpec(memory_space=pltpu.SMEM), vmem],
         scratch_shapes=[pltpu.SMEM((slabs,), jnp.int32)],
+        compiler_params=pltpu.CompilerParams(vmem_limit_bytes=VMEM_BYTES),
         name="composite",
     )(layer_nearness_position, pieces)
 

time: 19.6 us -> 18.3 us (0.934)
  Pallas kernels: 3.38 us -> 2.31 us
  blocking collectives: 15.4 us -> 15.1 us
    pallas_call x1, Pallas kernels: 1.78 us -> 1.09 us  [body(): pl.pallas_call(functools.partial(march, step_rows, row_count, voxel_width...]
    pallas_call x1, Pallas kernels: 1.59 us -> 1.22 us  [body(): pl.pallas_call(functools.partial(composite, bricks, tiles, cores), out_sh...]
    all_to_all x1, blocking collectives: 15.4 us -> 15.1 us  [body(): lax.all_to_all(pieces, GROUP, split_axis=0, concat_axis=0, tiled=True)]
where the time goes in v1:
time: 18.3 us; the launch traced here: 18.1 us
  blocking collectives  15.1 us (83%)
  Pallas kernels  2.31 us (13%)
  between operations  0.65 us (4%)
    all_to_all x1, blocking collectives, body(): lax.all_to_all(pieces, GROUP, split_axis=0, concat_axis=0, tiled=True)  15.1 us
    pallas_call x1, Pallas kernels, body(): pl.pallas_call(functools.partial(composite, bricks, tiles, cores), out_sh...  1.22 us
    pallas_call x1, Pallas kernels, body(): pl.pallas_call(functools.partial(march, step_rows, row_count, voxel_width...  1.09 us

profile of v1, /device:TPU:0, one launch (start us, length us, event | category | flops | bytes accessed | tf_op | source)
XLA Modules:
  0.0 18.1 jit_solution(15249546327114727507)
XLA Ops:
  0.6 1.1 %march.1 = f32[16,8,256]{2,1,0:T(8,128)S(1)} custom-call(bf16[8,32,256]{2,1,0:T(8,128)(2,1)} %soot_hbm.1, bf16[8,32,256]{2,1,0:T(8,128)(2,1)} %warmth_hbm.1), custom_call_target="tpu_custom_call" | custom-call | tf_op jit(solution)/shard_map/march/pallas_call | solution.py:105
  1.7 0.0 copy-start
  1.7 15.1 %all_to_all.5.pieces_ref = f32[16,8,256]{2,1,0:T(8,128)S(1)} all-to-all(f32[16,8,256]{2,1,0:T(8,128)S(1)} %march.1), channel_id=1, replica_groups=mesh['parts'=2,'brick'=4,'tile'=2,'depth'=2] {'brick','tile','depth'}, dimensions={0} | all-to-all | bytes 262144 | tf_op jit(solution)/shard_map/all_to_all | solution.py:121
  16.8 0.0 copy-done
  16.8 1.2 %composite.1 = (f32[3,2,512]{2,1,0:T(2,128)}, f32[2,512]{1,0:T(2,128)}) custom-call(s32[8]{0:T(128)S(1)} %copy-done, f32[16,8,256]{2,1,0:T(8,128)S(1)} %all_to_all.5.pieces_ref), custom_call_target="tpu_custom_call" | custom-call | tf_op jit(solution)/shard_map/composite/pallas_call | solution.py:122
Async XLA Ops:
  1.7 15.1 %copy-start = (s32[8]{0:T(128)S(1)}, s32[8]{0:T(128)}, u32[]{:S(2)}) copy-start(s32[8]{0:T(128)} %position_ref.1) | copy-start | bytes 100

commit v2 on v1

--- a/solution.py
+++ b/solution.py
@@ -12,7 +12,24 @@
 VMEM_BYTES = 24 << 20
 
 
-def march(step_rows, row_count, voxel_width, soot_hbm, warmth_hbm, out_ref, soot_ref, warmth_ref, arrived):
+def seat(sizes, member):
+    place = 0
+    for size, at in zip(sizes, member):
+        place = place * size + (at + size - size // 2) % size
+    return place
+
+
+def coordinates(sizes, index):
+    bricks, tiles, cores = sizes
+    return index // (tiles * cores), index // cores % tiles, index % cores
+
+
+def seating(sizes):
+    members = range(sizes[0] * sizes[1] * sizes[2])
+    return sorted(members, key=lambda index: seat(sizes, coordinates(sizes, index)))
+
+
+def march(sizes, step_rows, row_count, voxel_width, soot_hbm, warmth_hbm, out_ref, soot_ref, warmth_ref, arrived):
     layers, rows, width = soot_ref.shape
     steps = rows // step_rows
 
@@ -52,8 +69,9 @@
         fields = [2.0 * radiance[0], 2.0 * radiance[1], 2.0 * radiance[2], transmit]
         owners = step_rows // row_count
         for owner in range(owners):
+            place = seat(sizes, coordinates(sizes, index * owners + owner))
             for c in range(4):
-                out_ref[index * owners + owner, c * row_count : (c + 1) * row_count, :] = fields[c][
+                out_ref[place, c * row_count : (c + 1) * row_count, :] = fields[c][
                     owner * row_count : (owner + 1) * row_count, :
                 ]
         return carry
@@ -62,7 +80,8 @@
     lax.fori_loop(0, steps, strip, 0, unroll=steps <= 4)
 
 
-def composite(bricks, tiles, cores, position_ref, pieces_ref, colour_ref, opacity_ref, slab_at):
+def composite(sizes, position_ref, pieces_ref, colour_ref, opacity_ref, slab_at):
+    bricks, tiles, cores = sizes
     slabs = bricks * cores
     row_count, width = pieces_ref.shape[1] // 4, pieces_ref.shape[2]
 
@@ -76,7 +95,7 @@
         def add(p, state):
             colour, through = state
             slab = slab_at[p]
-            piece = pieces_ref[((slab // cores) * tiles + tile) * cores + slab % cores]
+            piece = pieces_ref[seat(sizes, (slab // cores, tile, slab % cores))]
             colour = [
                 colour[c] + piece[c * row_count : (c + 1) * row_count] * through for c in range(3)
             ]
@@ -94,7 +113,8 @@
 
 
 def body(soot_extinction, scaled_warmth, layer_nearness_position):
-    bricks, tiles, cores = (lax.axis_size(name) for name in GROUP)
+    sizes = tuple(lax.axis_size(name) for name in GROUP)
+    bricks, tiles, cores = sizes
     layers, rows, width = soot_extinction.shape
     slabs, owners = bricks * cores, bricks * tiles * cores
     row_count = rows // owners
@@ -103,7 +123,7 @@
     vmem = pl.BlockSpec(memory_space=pltpu.VMEM)
     step_rows = min(STEP_ROWS, rows)
     pieces = pl.pallas_call(
-        functools.partial(march, step_rows, row_count, voxel_width),
+        functools.partial(march, sizes, step_rows, row_count, voxel_width),
         out_shape=jax.ShapeDtypeStruct((owners, 4 * row_count, width), jnp.float32),
         in_specs=[hbm, hbm],
         out_specs=vmem,
@@ -118,9 +138,11 @@
         pltpu.with_memory_space_constraint(soot_extinction, pltpu.HBM),
         pltpu.with_memory_space_constraint(scaled_warmth, pltpu.HBM),
     )
-    pieces = lax.all_to_all(pieces, GROUP, split_axis=0, concat_axis=0, tiled=True)
+    pieces = lax.all_to_all(
+        pieces, GROUP, 0, 0, axis_index_groups=[seating(sizes)], tiled=True
+    )
     return pl.pallas_call(
-        functools.partial(composite, bricks, tiles, cores),
+        functools.partial(composite, sizes),
         out_shape=(
             jax.ShapeDtypeStruct((3, row_count, tiles * width), jnp.float32),
             jax.ShapeDtypeStruct((row_count, tiles * width), jnp.float32),

time: 18.3 us -> 14.4 us (0.79)
  the two profiles are of different devices: /device:TPU:0 before, /device:TPU:1 now
where the time goes in v2:
time: 14.4 us; the launch traced here: 14.2 us
  blocking collectives  11.1 us (77%)
  Pallas kernels  2.43 us (17%)
  between operations  0.65 us (5%)
    all_to_all x1, blocking collectives, body(): lax.all_to_all(pieces, GROUP, 0, 0, axis_index_groups=[seating(sizes)], t...  11.1 us
    pallas_call x1, Pallas kernels, body(): pl.pallas_call(functools.partial(composite, sizes), out_shape=(jax.ShapeD...  1.33 us
    pallas_call x1, Pallas kernels, body(): pl.pallas_call(functools.partial(march, sizes, step_rows, row_count, voxe...  1.09 us

profile of v2, /device:TPU:1, one launch (start us, length us, event | category | flops | bytes accessed | tf_op | source)
XLA Modules:
  0.0 14.2 jit_solution(14796710343416261380)
XLA Ops:
  0.6 1.1 %march.1 = f32[16,8,256]{2,1,0:T(8,128)S(1)} custom-call(bf16[8,32,256]{2,1,0:T(8,128)(2,1)} %soot_hbm.1, bf16[8,32,256]{2,1,0:T(8,128)(2,1)} %warmth_hbm.1), custom_call_target="tpu_custom_call" | custom-call | tf_op jit(solution)/shard_map/march/pallas_call | solution.py:125
  1.7 0.0 copy-start
  1.7 11.1 %all_to_all.5.pieces_ref = f32[16,8,256]{2,1,0:T(8,128)S(1)} all-to-all(f32[16,8,256]{2,1,0:T(8,128)S(1)} %march.1), channel_id=1, replica_groups={{11,10,9,8,15,14,13,12,3,2,1,0,7,6,5,4},{27,26,25,24,31,30,29,28,19,18,..., dimensions={0} | all-to-all | bytes 262144 | tf_op jit(solution)/shard_map/all_to_all | solution.py:141
  12.8 0.0 copy-done
  12.8 1.3 %composite.1 = (f32[3,2,512]{2,1,0:T(2,128)}, f32[2,512]{1,0:T(2,128)}) custom-call(s32[8]{0:T(128)S(1)} %copy-done, f32[16,8,256]{2,1,0:T(8,128)S(1)} %all_to_all.5.pieces_ref), custom_call_target="tpu_custom_call" | custom-call | tf_op jit(solution)/shard_map/composite/pallas_call | solution.py:144
Async XLA Ops:
  1.7 11.1 %copy-start = (s32[8]{0:T(128)S(1)}, s32[8]{0:T(128)}, u32[]{:S(2)}) copy-start(s32[8]{0:T(128)} %position_ref.1) | copy-start | bytes 100
